TPU v7x, 256 devices: a whole 4x4x8 slice. The times are simulated.
256 devices in a mesh: rows: 128 (over z, x, y), half: 2 (over core).
Axes of the slice: x: 4, y: 4, z: 8, core: 2. Of those that a mesh axis runs over, the one named last changes fastest.
Arguments:
- source_feats: bfloat16 [131072, 1024], P('rows', 'half'), may hold values from -6 to 6
- rel_weight: bfloat16 [3, 2, 512, 512], P(None, 'half'), may hold values from -0.25 to 0.25
- tiles: bfloat16 [4096, 64, 512], P('rows'), may hold values from -0.25 to 0.25
- src_blk: int32 [4096, 8], P('rows'), may hold values from 0 to 15
- rel_id: int32 [4096, 8], P('rows'), may hold values from 0 to 2
- owner: int32 [4096, 1], P('rows'), may hold values from 0 to 127; in each aligned block of 32 rows (0 to 31, 32 to 63, ...) at most 2 rows name the same one
- local_blk: int32 [4096], P('rows'), may hold values from 0 to 31
- in_degree: int32 [262144], P('rows'), may hold values from 1 to 16
- mix_weight: bfloat16 [1024, 1024], P(None, 'half'), may hold values from -0.1875 to 0.1875
- bias: float32 [1024], P('half'), may hold values from -0.5 to 0.5
Outputs:
- out: bfloat16 [262144, 1024], P('rows', 'half')
Inputs may be any that keep to these rules, and one draw needn't show every extreme that they name: Among the 32 rows held by one device along rows, no owner is named more than 2 times, some owner exactly 2 times, and every owner is named somewhere.
All inputs are finite; a program needn't handle non-finite values.
Results may differ from a plain program's by a relative error of at most 0.0054.
Values may be sent and summed in bfloat16 or wider, within the bound.
A program may use at most 128 MiB of HBM per device.

v0:
```python
import jax
import jax.numpy as jnp
from jax import lax
from jax.sharding import PartitionSpec as P


def local(
    source_feats, rel_weight, tiles, src_blk, rel_id, owner, local_blk, in_degree, mix_weight, bias
):
    n_rows = lax.axis_size("rows")
    src_dev, half_w = source_feats.shape
    tile = tiles.shape[1]
    parts, per_row = src_blk.shape
    n_rel = rel_weight.shape[0]
    n_src_blocks = src_dev // tile
    n_blocks = n_rel * n_src_blocks
    n_local = in_degree.shape[0] // tile
    capacity = max(2, 2 * parts // n_rows)
    msgs = jnp.einsum(
        "sj,rjc->rsc", source_feats, rel_weight[:, 0], preferred_element_type=jnp.float32
    ).astype(jnp.bfloat16)
    flat_blocks = msgs.reshape(n_blocks, tile * half_w)
    picks = rel_id * n_src_blocks + src_blk
    per_turn = 16
    block_ids = jnp.arange(n_blocks, dtype=jnp.int32)

    def partial_group(operands):
        group_tiles, group_picks = operands
        chooser = (group_picks.reshape(per_turn * per_row)[:, None] == block_ids[None, :]).astype(
            jnp.bfloat16
        )
        picked = jnp.dot(chooser, flat_blocks, preferred_element_type=jnp.float32).astype(
            jnp.bfloat16
        )
        picked = picked.reshape(per_turn, per_row * tile, half_w)
        return jnp.einsum(
            "pim,pmc->pic", group_tiles, picked, preferred_element_type=jnp.float32
        ).astype(jnp.bfloat16)

    grouped = (
        tiles.reshape(parts // per_turn, per_turn, tile, per_row * tile),
        picks.reshape(parts // per_turn, per_turn, per_row),
    )
    partials = lax.map(partial_group, grouped).reshape(parts, tile * half_w)
    target_dev = owner[:, 0]
    positions = jnp.arange(parts, dtype=jnp.int32)
    earlier = (target_dev[:, None] == target_dev[None, :]) & (
        positions[None, :] < positions[:, None]
    )
    rank = jnp.sum(earlier.astype(jnp.int32), axis=1)
    slot = target_dev * capacity + rank
    slot_ids = jnp.arange(n_rows * capacity, dtype=jnp.int32)
    placing = slot_ids[:, None] == slot[None, :]
    outgoing = jnp.dot(
        placing.astype(jnp.bfloat16), partials, preferred_element_type=jnp.float32
    ).astype(jnp.bfloat16)
    out_ids = jnp.sum(jnp.where(placing, local_blk[None, :] + 1, 0), axis=1) - 1
    block_index = jnp.arange(n_local, dtype=jnp.int32)
    arrived, arrived_ids = (
        lax.all_to_all(outgoing, "rows", split_axis=0, concat_axis=0, tiled=True),
        lax.all_to_all(out_ids, "rows", split_axis=0, concat_axis=0, tiled=True),
    )
    selector = (arrived_ids[None, :] == block_index[:, None]).astype(jnp.bfloat16)
    summed = jnp.dot(selector, arrived, preferred_element_type=jnp.float32)
    summed = summed.reshape(n_local * tile, half_w)
    agg = (summed / in_degree.astype(jnp.float32)[:, None]).astype(jnp.bfloat16)
    mixed = jnp.dot(
        lax.all_gather(agg, "half", axis=1, tiled=True),
        mix_weight,
        preferred_element_type=jnp.float32,
    )
    return jax.nn.relu(mixed + bias).astype(jnp.bfloat16)


def solution(mesh):
    placed = (
        P("rows", "half"),
        P(None, "half", None, None),
        P("rows", None, None),
        P("rows", None),
        P("rows", None),
        P("rows", None),
        P("rows"),
        P("rows"),
        P(None, "half"),
        P("half"),
    )
    return jax.shard_map(
        local, mesh=mesh, in_specs=placed, out_specs=P("rows", "half"), check_vma=False
    )
```

profile of v0, /device:TPU:1, one launch (start us, length us, event | category | flops | bytes accessed | tf_op | source)
XLA Modules:
  0.0 598.6 jit_solution(10182642154321596765)
XLA Ops:
  6.5 0.0 copy-start
  6.5 1.0 convert_reduce_fusion
  7.5 0.7 multiply_add_fusion.1
  8.2 0.1 select_reduce_fusion
  8.3 0.8 sub.7
  9.0 16.3 %all-to-all-start = ((s32[128,2,1]{1,2,0:T(1,128)}), s32[128,2,1]{1,2,0:T(1,128)S(1)}, u32[]{:S(2)}, u32[]{:S(2)}) async-start(s32[128,2,1]{1,2,0:T(1,128)} %bitcast.1), calls=%async_computation | async-start | bytes 131072 | tf_op jit(solution)/shard_map/all_to_all | solution.py:61
  25.4 0.0 copy-done
  25.4 4.8 convert_bitcast_fusion
  30.2 4.7 copy.23
  34.8 0.0 copy-start.3
  34.8 0.0 copy-start.4
  34.8 5.9 reshape.55
  40.7 0.0 copy-done.3
  40.7 0.0 copy-done.4
  40.7 0.1 copy.21
  40.8 54.5 %while.11 = (s32[]{:T(128)}, bf16[2,16,64,512]{3,2,1,0:T(8,128)(2,1)}, bf16[2,16,64,512]{3,2,1,0:T(8,128)(2,1)}, s32[2,16,8]{2,1,0:T(8,128)S(1)}, bf16[48,32768]{1,0:T(8,128)(2,1)}, /*index=5*/s32[]{:T(128)}) while((s32[]{:T(128)}, bf16[2,16,64,512]{3,2,1,0:T(8,128)(2,1)}, bf16[2,16,64,512]{3,2,1,0:T(8,128)(2,1)}, ...), condition=%wide.region_3.4_spmd.clone, body=%wide.region_2.3_spmd.clone.sunk | while | flops 944248832 | bytes 38800968 | solution.py:44
  40.8 0.1 eq.105
  40.9 7.5 %convolution_convert_fusion.4 = bf16[128,32768]{1,0:T(8,128)(2,1)} fusion(bf16[48,32768]{1,0:T(8,128)(2,1)} %get-tuple-element.109, s32[128]{0:T(128)S(1)} %eq.105), kind=kOutput, calls=%fused_computation.1.clone.1 | convolution fusion | flops 406853632 | bytes 11534848 | tf_op jit(solution)/shard_map/while/body/eval_jaxpr/dot_general | solution.py:32
  48.4 13.5 %reshape.70 = bf16[16,512,512]{2,1,0:T(8,128)(2,1)} reshape(bf16[128,32768]{1,0:T(8,128)(2,1)} %convolution_convert_fusion.4) | data formatting | bytes 16777216 | tf_op jit(solution)/shard_map/while/body/eval_jaxpr/reshape | solution.py:35
  61.9 6.1 %fusion.27 = bf16[2,16,64,512]{3,2,1,0:T(8,128)(2,1)} fusion(bf16[2,16,64,512]{3,2,1,0:T(8,128)(2,1)} %get-tuple-element.100, s32[]{:T(128)} %get-tuple-element.99, bf16[16,512,512]{2,1,0:T(8,128)(2,1)} %reshape.70, bf16[2,16,64,512]{3,2,1,0:T(8,128)(2,1)} %get-tuple-element.107), kind=kOutput, calls=%fused_computation.4.clone.1 | convolution fusion | flops 537395200 | bytes 10486784 | tf_op jit(solution)/shard_map/while/body/eval_jaxpr/pim,pmc->pic/dot_general | solution.py:36
  68.0 0.1 eq.105
  68.1 7.5 %convolution_convert_fusion.4 = bf16[128,32768]{1,0:T(8,128)(2,1)} fusion(bf16[48,32768]{1,0:T(8,128)(2,1)} %get-tuple-element.109, s32[128]{0:T(128)S(1)} %eq.105), kind=kOutput, calls=%fused_computation.1.clone.1 | convolution fusion | flops 406853632 | bytes 11534848 | tf_op jit(solution)/shard_map/while/body/eval_jaxpr/dot_general | solution.py:32
  75.6 13.5 %reshape.70 = bf16[16,512,512]{2,1,0:T(8,128)(2,1)} reshape(bf16[128,32768]{1,0:T(8,128)(2,1)} %convolution_convert_fusion.4) | data formatting | bytes 16777216 | tf_op jit(solution)/shard_map/while/body/eval_jaxpr/reshape | solution.py:35
  89.1 6.2 %fusion.27 = bf16[2,16,64,512]{3,2,1,0:T(8,128)(2,1)} fusion(bf16[2,16,64,512]{3,2,1,0:T(8,128)(2,1)} %get-tuple-element.100, s32[]{:T(128)} %get-tuple-element.99, bf16[16,512,512]{2,1,0:T(8,128)(2,1)} %reshape.70, bf16[2,16,64,512]{3,2,1,0:T(8,128)(2,1)} %get-tuple-element.107), kind=kOutput, calls=%fused_computation.4.clone.1 | convolution fusion | flops 537395200 | bytes 10486784 | tf_op jit(solution)/shard_map/while/body/eval_jaxpr/pim,pmc->pic/dot_general | solution.py:36
  95.3 2.8 copy.25
  98.0 8.2 %convolution_convert_fusion.2 = bf16[256,32768]{1,0:T(8,128)(2,1)} fusion(bf16[32,32768]{1,0:T(8,128)(2,1)S(1)} %bitcast.39, s32[32]{0:T(128)S(1)} %get-tuple-element.60), kind=kOutput, calls=%fused_computation.11 | convolution fusion | flops 545267712 | bytes 18874496 | tf_op jit(solution)/shard_map/dot_general | solution.py:54
  106.2 27.0 %all_to_all.13 = bf16[128,2,32768]{2,1,0:T(2,128)(2,1)} reshape(bf16[256,32768]{1,0:T(8,128)(2,1)} %convolution_convert_fusion.2) | data formatting | bytes 33554432 | tf_op jit(solution)/shard_map/all_to_all | solution.py:60
  133.2 0.0 copy-start.2
  133.2 0.0 all-to-all-done
  133.2 14.0 %all-to-all-start.1 = ((bf16[128,2,32768]{2,1,0:T(2,128)(2,1)}), bf16[128,2,32768]{2,1,0:T(2,128)(2,1)}, u32[]{:S(2)}, u32[]{:S(2)}) async-start(bf16[128,2,32768]{2,1,0:T(2,128)(2,1)} %all_to_all.13), calls=%async_computation.1 | async-start | bytes 33554432 | tf_op jit(solution)/shard_map/all_to_all | solution.py:60
  147.2 0.0 all-gather.2.cloned.1.call-start
  147.2 0.0 copy-done.2
  147.3 0.5 broadcast.26
  147.8 0.8 reduce.3
  148.6 0.1 eq.62
  148.7 376.1 %all-to-all-done.1 = bf16[128,2,32768]{2,1,0:T(2,128)(2,1)} async-done(((bf16[128,2,32768]{2,1,0:T(2,128)(2,1)}), bf16[128,2,32768]{2,1,0:T(2,128)(2,1)}, u32[]{:S(2)}, u32[]{:S(2)}) %all-to-all-start.1) | async-done | bytes 16777248 | tf_op jit(solution)/shard_map/all_to_all | solution.py:60
  524.8 25.0 %all_to_all.15 = bf16[256,32768]{1,0:T(8,128)(2,1)} reshape(bf16[128,2,32768]{2,1,0:T(2,128)(2,1)} %all-to-all-done.1) | data formatting | bytes 33554432 | tf_op jit(solution)/shard_map/all_to_all | solution.py:60
  549.8 10.6 %fusion.10 = f32[32,32768]{1,0:T(8,128)} fusion(bf16[256,32768]{1,0:T(8,128)(2,1)} %all_to_all.15, s32[256]{0:T(256)S(1)} %eq.62), kind=kOutput, calls=%fused_computation.20 | convolution fusion | flops 536879104 | bytes 20972544 | tf_op jit(solution)/shard_map/dot_general | solution.py:64
  560.4 4.9 reshape.57
  565.3 0.0 copy-start.5
  565.3 0.0 copy-start.6
  565.3 4.0 divide_convert_fusion
  569.3 0.0 all-gather.2.cloned.1.call-update
  569.3 16.5 %all-gather.2.cloned.1.call-done = bf16[2048,1024]{1,0:T(8,128)(2,1)} async-done(((bf16[2048,512]{1,0:T(8,128)(2,1)}), bf16[2048,1024]{1,0:T(8,128)(2,1)}) %all-gather.2.cloned.1.call-update) | async-done | bytes 4194320 | tf_op jit(solution)/shard_map/all_gather | solution.py:68
  585.8 0.0 copy-done.5
  585.8 0.0 copy-done.6
  585.8 0.0 copy-start.1
  585.8 6.0 maximum_convert_fusion
  591.8 0.0 copy-done.1
  (6 shorter events, 0.0 us)
Async XLA Ops:
  6.5 18.9 %copy-start = (bf16[3,1,512,512]{3,2,1,0:T(8,128)(2,1)S(1)}, bf16[3,1,512,512]{3,2,1,0:T(8,128)(2,1)}, u32[]{:S(2)}) copy-start(bf16[3,1,512,512]{3,2,1,0:T(8,128)(2,1)} %param.13) | copy-start | bytes 4718596
  9.0 124.1 %all-to-all-start = ((s32[128,2,1]{1,2,0:T(1,128)}), s32[128,2,1]{1,2,0:T(1,128)S(1)}, u32[]{:S(2)}, u32[]{:S(2)}) async-start(s32[128,2,1]{1,2,0:T(1,128)} %bitcast.1), calls=%async_computation | async-start | bytes 131072 | tf_op jit(solution)/shard_map/all_to_all | solution.py:61
  34.8 5.9 copy-start.3
  34.8 5.9 copy-start.4
  133.2 14.1 %copy-start.2 = (s32[2048]{0:T(1024)S(1)}, s32[2048]{0:T(1024)}, u32[]{:S(2)}) copy-start(s32[2048]{0:T(1024)} %param.19) | copy-start | bytes 24580
  133.2 391.7 %all-to-all-start.1 = ((bf16[128,2,32768]{2,1,0:T(2,128)(2,1)}), bf16[128,2,32768]{2,1,0:T(2,128)(2,1)}, u32[]{:S(2)}, u32[]{:S(2)}) async-start(bf16[128,2,32768]{2,1,0:T(2,128)(2,1)} %all_to_all.13), calls=%async_computation.1 | async-start | bytes 33554432 | tf_op jit(solution)/shard_map/all_to_all | solution.py:60
  147.2 438.6 %all-gather.2.cloned.1.call-start = ((), (), s32[]{:S(2)}) async-start(), calls=%async_computation.2 | async-start | bytes 6291456 | tf_op jit(solution)/shard_map/all_gather | solution.py:68
  565.3 20.5 %copy-start.5 = (bf16[1024,512]{1,0:T(8,128)(2,1)S(1)}, bf16[1024,512]{1,0:T(8,128)(2,1)}, u32[]{:S(2)}) copy-start(bf16[1024,512]{1,0:T(8,128)(2,1)} %param.20) | copy-start | bytes 3145732
  565.3 20.5 %copy-start.6 = (f32[512]{0:T(512)S(1)}, f32[512]{0:T(512)}, u32[]{:S(2)}) copy-start(f32[512]{0:T(512)} %param.21) | copy-start | bytes 6148
  585.8 6.0 copy-start.1
Sparse Core Ops, SparseCore 0:
  569.4 16.2 all-gather.1
where the time goes:
time: 601 us; the launch traced here: 599 us
  waiting for transfers between devices  393 us (65%)
  local copies, waits for them, and re-layouts  98.9 us (16%)
  matrix products  56.8 us (9%)
  starting transfers between devices  30.4 us (5%)
  between operations  13.5 us (2%)
  other arithmetic  6.52 us (1%)
    all_to_all x1, waiting for transfers between devices, local(): lax.all_to_all(outgoing, 'rows', split_axis=0, concat_axis=0, tiled=True)  376 us
    all_to_all x2, local copies, waits for them, and re-layouts, local(): lax.all_to_all(outgoing, 'rows', split_axis=0, concat_axis=0, tiled=True)  52 us
    reshape x2, local copies, waits for them, and re-layouts, partial_group(): picked = picked.reshape(per_turn, per_row * tile, half_w)  26.9 us
    all_gather x1, waiting for transfers between devices, local(): lax.all_gather(agg, 'half', axis=1, tiled=True)  16.5 us
    all_to_all x1, starting transfers between devices, local(): lax.all_to_all(out_ids, 'rows', split_axis=0, concat_axis=0, tiled=True)  16.3 us
    dot_general x2, matrix products, partial_group(): jnp.dot(chooser, flat_blocks, preferred_element_type=jnp.float32)  15 us
    all_to_all x1, starting transfers between devices, local(): lax.all_to_all(outgoing, 'rows', split_axis=0, concat_axis=0, tiled=True)  14 us
    dot_general x2, matrix products, partial_group(): jnp.einsum('pim,pmc->pic', group_tiles, picked, preferred_element_type=jn...  12.3 us
  transfers between devices with their start and end apart: 3, of which 2 were waited for; matrix products, arithmetic and copies ran while one was open for 14% of the time, Pallas kernels for 0%

commit v1 on v0

--- a/solution.py
+++ b/solution.py
@@ -65,7 +65,9 @@
     summed = summed.reshape(n_local * tile, half_w)
     agg = (summed / in_degree.astype(jnp.float32)[:, None]).astype(jnp.bfloat16)
     mixed = jnp.dot(
-        lax.all_gather(agg, "half", axis=1, tiled=True),
+        jnp.concatenate(
+            lax.all_to_all(jnp.stack([agg] * lax.axis_size("half")), "half", 0, 0), axis=1
+        ),
         mix_weight,
         preferred_element_type=jnp.float32,
     )

time: 601 us -> 582 us (0.968)
  waiting for transfers between devices: 393 us -> 376 us
  between operations: 13.5 us -> 0.11 us
  blocking collectives: 0 us -> 8.08 us
    all_gather x1 -> x0, waiting for transfers between devices: 16.5 us -> none  [local(): lax.all_gather(agg, 'half', axis=1, tiled=True)]
    all_to_all x0 -> x1, blocking collectives: none -> 8.08 us  [local(): lax.all_to_all(jnp.stack([agg] * lax.axis_size('half')), 'half', 0, 0)]
  transfers between devices with their start and end apart: 3 -> 2, of which waited for: 2 -> 1; matrix products, arithmetic and copies ran while one was open for 14% -> 14% of each run, Pallas kernels for 0% -> 0%
where the time goes in v1:
time: 582 us; the launch traced here: 579 us
  waiting for transfers between devices  376 us (65%)
  local copies, waits for them, and re-layouts  104 us (18%)
  matrix products  54.5 us (9%)
  starting transfers between devices  30.4 us (5%)
  blocking collectives  8.08 us (1%)
    all_to_all x1, waiting for transfers between devices, local(): lax.all_to_all(outgoing, 'rows', split_axis=0, concat_axis=0, tiled=True)  376 us
    all_to_all x2, local copies, waits for them, and re-layouts, local(): lax.all_to_all(outgoing, 'rows', split_axis=0, concat_axis=0, tiled=True)  52 us
    reshape x2, local copies, waits for them, and re-layouts, partial_group(): picked = picked.reshape(per_turn, per_row * tile, half_w)  26.9 us
    all_to_all x1, starting transfers between devices, local(): lax.all_to_all(out_ids, 'rows', split_axis=0, concat_axis=0, tiled=True)  16.3 us
    dot_general x2, matrix products, partial_group(): jnp.dot(chooser, flat_blocks, preferred_element_type=jnp.float32)  15 us
    all_to_all x1, starting transfers between devices, local(): lax.all_to_all(outgoing, 'rows', split_axis=0, concat_axis=0, tiled=True)  14 us
    dot_general x2, matrix products, partial_group(): jnp.einsum('pim,pmc->pic', group_tiles, picked, preferred_element_type=jn...  12.3 us
  transfers between devices with their start and end apart: 2, of which 1 were waited for; matrix products, arithmetic and copies ran while one was open for 14% of the time, Pallas kernels for 0%

profile of v1, /device:TPU:1, one launch (start us, length us, event | category | flops | bytes accessed | tf_op | source)
XLA Modules:
  0.0 579.2 jit_solution(13426691568418394700)
XLA Ops:
  0.0 0.0 copy-start
  0.0 1.0 convert_reduce_fusion
  1.0 0.7 multiply_add_fusion.1
  1.7 0.1 select_reduce_fusion
  1.8 0.8 sub.7
  2.5 16.3 %all-to-all-start = ((s32[128,2,1]{1,2,0:T(1,128)}), s32[128,2,1]{1,2,0:T(1,128)S(1)}, u32[]{:S(2)}, u32[]{:S(2)}) async-start(s32[128,2,1]{1,2,0:T(1,128)} %bitcast.1), calls=%async_computation | async-start | bytes 131072 | tf_op jit(solution)/shard_map/all_to_all | solution.py:61
  18.9 0.0 copy-done
  18.9 4.8 convert_bitcast_fusion
  23.6 4.7 copy.25
  28.3 0.0 copy-start.3
  28.3 0.0 copy-start.4
  28.3 5.9 %reshape.91 = bf16[48,32768]{1,0:T(8,128)(2,1)} reshape(bf16[3,1024,512]{2,1,0:T(8,128)(2,1)} %copy.25) | data formatting | bytes 6291456 | tf_op jit(solution)/shard_map/reshape | solution.py:22
  34.3 0.0 copy-done.3
  34.3 0.0 copy-done.4
  34.3 0.1 copy.23
  34.3 54.4 %while.11 = (s32[]{:T(128)}, bf16[2,16,64,512]{3,2,1,0:T(8,128)(2,1)}, bf16[2,16,64,512]{3,2,1,0:T(8,128)(2,1)}, s32[2,16,8]{2,1,0:T(8,128)S(1)}, bf16[48,32768]{1,0:T(8,128)(2,1)}, /*index=5*/s32[]{:T(128)}) while((s32[]{:T(128)}, bf16[2,16,64,512]{3,2,1,0:T(8,128)(2,1)}, bf16[2,16,64,512]{3,2,1,0:T(8,128)(2,1)}, ...), condition=%wide.region_3.4_spmd.clone, body=%wide.region_2.3_spmd.clone.sunk | while | flops 944248832 | bytes 38800968 | solution.py:44
  34.4 0.1 eq.105
  34.4 7.5 %convolution_convert_fusion.4 = bf16[128,32768]{1,0:T(8,128)(2,1)} fusion(bf16[48,32768]{1,0:T(8,128)(2,1)} %get-tuple-element.109, s32[128]{0:T(128)S(1)} %eq.105), kind=kOutput, calls=%fused_computation.1.clone.1 | convolution fusion | flops 406853632 | bytes 11534848 | tf_op jit(solution)/shard_map/while/body/eval_jaxpr/dot_general | solution.py:32
  41.9 13.5 %reshape.108 = bf16[16,512,512]{2,1,0:T(8,128)(2,1)} reshape(bf16[128,32768]{1,0:T(8,128)(2,1)} %convolution_convert_fusion.4) | data formatting | bytes 16777216 | tf_op jit(solution)/shard_map/while/body/eval_jaxpr/reshape | solution.py:35
  55.4 6.1 %fusion.27 = bf16[2,16,64,512]{3,2,1,0:T(8,128)(2,1)} fusion(bf16[2,16,64,512]{3,2,1,0:T(8,128)(2,1)} %get-tuple-element.100, s32[]{:T(128)} %get-tuple-element.99, bf16[16,512,512]{2,1,0:T(8,128)(2,1)} %reshape.108, bf16[2,16,64,512]{3,2,1,0:T(8,128)(2,1)} %get-tuple-element.107), kind=kOutput, calls=%fused_computation.4.clone.1 | convolution fusion | flops 537395200 | bytes 10486784 | tf_op jit(solution)/shard_map/while/body/eval_jaxpr/pim,pmc->pic/dot_general | solution.py:36
  61.5 0.1 eq.105
  61.6 7.5 %convolution_convert_fusion.4 = bf16[128,32768]{1,0:T(8,128)(2,1)} fusion(bf16[48,32768]{1,0:T(8,128)(2,1)} %get-tuple-element.109, s32[128]{0:T(128)S(1)} %eq.105), kind=kOutput, calls=%fused_computation.1.clone.1 | convolution fusion | flops 406853632 | bytes 11534848 | tf_op jit(solution)/shard_map/while/body/eval_jaxpr/dot_general | solution.py:32
  69.1 13.5 %reshape.108 = bf16[16,512,512]{2,1,0:T(8,128)(2,1)} reshape(bf16[128,32768]{1,0:T(8,128)(2,1)} %convolution_convert_fusion.4) | data formatting | bytes 16777216 | tf_op jit(solution)/shard_map/while/body/eval_jaxpr/reshape | solution.py:35
  82.6 6.1 %fusion.27 = bf16[2,16,64,512]{3,2,1,0:T(8,128)(2,1)} fusion(bf16[2,16,64,512]{3,2,1,0:T(8,128)(2,1)} %get-tuple-element.100, s32[]{:T(128)} %get-tuple-element.99, bf16[16,512,512]{2,1,0:T(8,128)(2,1)} %reshape.108, bf16[2,16,64,512]{3,2,1,0:T(8,128)(2,1)} %get-tuple-element.107), kind=kOutput, calls=%fused_computation.4.clone.1 | convolution fusion | flops 537395200 | bytes 10486784 | tf_op jit(solution)/shard_map/while/body/eval_jaxpr/pim,pmc->pic/dot_general | solution.py:36
  88.7 2.8 copy.28
  91.5 8.2 %convolution_convert_fusion.2 = bf16[256,32768]{1,0:T(8,128)(2,1)} fusion(bf16[32,32768]{1,0:T(8,128)(2,1)S(1)} %bitcast.42, s32[32]{0:T(128)S(1)} %get-tuple-element.60), kind=kOutput, calls=%fused_computation.11 | convolution fusion | flops 545267712 | bytes 18874496 | tf_op jit(solution)/shard_map/dot_general | solution.py:54
  99.7 27.0 %all_to_all.16 = bf16[128,2,32768]{2,1,0:T(2,128)(2,1)} reshape(bf16[256,32768]{1,0:T(8,128)(2,1)} %convolution_convert_fusion.2) | data formatting | bytes 33554432 | tf_op jit(solution)/shard_map/all_to_all | solution.py:60
  126.7 0.0 copy-start.2
  126.7 0.0 all-to-all-done
  126.7 14.0 %all-to-all-start.1 = ((bf16[128,2,32768]{2,1,0:T(2,128)(2,1)}), bf16[128,2,32768]{2,1,0:T(2,128)(2,1)}, u32[]{:S(2)}, u32[]{:S(2)}) async-start(bf16[128,2,32768]{2,1,0:T(2,128)(2,1)} %all_to_all.16), calls=%async_computation.1 | async-start | bytes 33554432 | tf_op jit(solution)/shard_map/all_to_all | solution.py:60
  140.7 0.0 copy-done.2
  140.7 0.5 broadcast.40
  141.2 0.8 reduce.3
  142.1 0.1 eq.62
  142.2 376.1 %all-to-all-done.1 = bf16[128,2,32768]{2,1,0:T(2,128)(2,1)} async-done(((bf16[128,2,32768]{2,1,0:T(2,128)(2,1)}), bf16[128,2,32768]{2,1,0:T(2,128)(2,1)}, u32[]{:S(2)}, u32[]{:S(2)}) %all-to-all-start.1) | async-done | bytes 16777248 | tf_op jit(solution)/shard_map/all_to_all | solution.py:60
  518.3 25.0 %all_to_all.18 = bf16[256,32768]{1,0:T(8,128)(2,1)} reshape(bf16[128,2,32768]{2,1,0:T(2,128)(2,1)} %all-to-all-done.1) | data formatting | bytes 33554432 | tf_op jit(solution)/shard_map/all_to_all | solution.py:60
  543.3 10.6 %fusion.10 = f32[32,32768]{1,0:T(8,128)} fusion(bf16[256,32768]{1,0:T(8,128)(2,1)} %all_to_all.18, s32[256]{0:T(256)S(1)} %eq.62), kind=kOutput, calls=%fused_computation.21 | convolution fusion | flops 536879104 | bytes 20972544 | tf_op jit(solution)/shard_map/dot_general | solution.py:64
  553.9 4.9 reshape.93
  558.8 5.5 copy.26
  564.3 2.7 divide_convert_fusion
  567.0 0.4 pad_maximum_fusion
  567.4 0.0 copy-start.5
  567.4 0.0 copy-start.6
  567.4 8.1 %all_to_all.23 = bf16[2,2048,512]{1,2,0:T(8,128)(2,1)S(1)} all-to-all(bf16[2,2048,512]{1,2,0:T(8,128)(2,1)S(1)} %pad_maximum_fusion), channel_id=1, replica_groups=mesh['rows'=128,'half'=2] {'half'}, dimensions={0} | all-to-all | bytes 8388608 | tf_op jit(solution)/shard_map/all_to_all | solution.py:69
  575.5 0.0 copy-start.1
  575.5 0.0 copy-done.5
  575.5 0.0 copy-done.6
  575.5 3.8 maximum_convert_fusion
  579.2 0.0 copy-done.1
  (6 shorter events, 0.0 us)
Async XLA Ops:
  0.0 18.9 %copy-start = (bf16[3,1,512,512]{3,2,1,0:T(8,128)(2,1)S(1)}, bf16[3,1,512,512]{3,2,1,0:T(8,128)(2,1)}, u32[]{:S(2)}) copy-start(bf16[3,1,512,512]{3,2,1,0:T(8,128)(2,1)} %param.13) | copy-start | bytes 4718596
  2.5 124.1 %all-to-all-start = ((s32[128,2,1]{1,2,0:T(1,128)}), s32[128,2,1]{1,2,0:T(1,128)S(1)}, u32[]{:S(2)}, u32[]{:S(2)}) async-start(s32[128,2,1]{1,2,0:T(1,128)} %bitcast.1), calls=%async_computation | async-start | bytes 131072 | tf_op jit(solution)/shard_map/all_to_all | solution.py:61
  28.3 5.9 %copy-start.3 = (s32[32,8]{0,1:T(8,128)S(1)}, s32[32,8]{0,1:T(8,128)}, u32[]{:S(2)}) copy-start(s32[32,8]{0,1:T(8,128)} %param.15) | copy-start | bytes 3076
  28.3 5.9 %copy-start.4 = (s32[32,8]{0,1:T(8,128)S(1)}, s32[32,8]{0,1:T(8,128)}, u32[]{:S(2)}) copy-start(s32[32,8]{0,1:T(8,128)} %param.16) | copy-start | bytes 3076
  126.7 14.1 %copy-start.2 = (s32[2048]{0:T(1024)S(1)}, s32[2048]{0:T(1024)}, u32[]{:S(2)}) copy-start(s32[2048]{0:T(1024)} %param.19) | copy-start | bytes 24580
  126.7 391.6 %all-to-all-start.1 = ((bf16[128,2,32768]{2,1,0:T(2,128)(2,1)}), bf16[128,2,32768]{2,1,0:T(2,128)(2,1)}, u32[]{:S(2)}, u32[]{:S(2)}) async-start(bf16[128,2,32768]{2,1,0:T(2,128)(2,1)} %all_to_all.16), calls=%async_computation.1 | async-start | bytes 33554432 | tf_op jit(solution)/shard_map/all_to_all | solution.py:60
  567.4 8.1 %copy-start.5 = (bf16[1024,512]{1,0:T(8,128)(2,1)S(1)}, bf16[1024,512]{1,0:T(8,128)(2,1)}, u32[]{:S(2)}) copy-start(bf16[1024,512]{1,0:T(8,128)(2,1)} %param.20) | copy-start | bytes 3145732
  567.4 8.1 %copy-start.6 = (f32[512]{0:T(512)S(1)}, f32[512]{0:T(512)}, u32[]{:S(2)}) copy-start(f32[512]{0:T(512)} %param.21) | copy-start | bytes 6148
  575.5 3.8 copy-start.1
